TPU v7x, 128 devices: a whole 4x4x4 slice. The times are simulated.
128 devices in a mesh: row: 8 (over y_lo, x), col: 16 (over y_hi, z, core).
Axes of the slice: x: 4, y: 4 (y_hi: 2, y_lo: 2; y = y_hi * 2 + y_lo), z: 4, core: 2. Of those that a mesh axis runs over, the one named last changes fastest.
Arguments:
- factor_panel: bfloat16 [12288, 98304], P('row', 'col'), may hold values from -1 to 1, as said below
- normals: bfloat16 [98304, 128], P(('col', 'row')), may hold values from -6 to 6
- bond_vectors: float32 [3, 4096, 12], P(None, ('col', 'row')), may hold values from -9 to 9
- neighbours: int32 [4096, 12], P(('col', 'row')), may hold values from 0 to 175
- send_atoms: int32 [128, 16], P(('col', 'row')), may hold values from 0 to 31
- radial_weight: bfloat16 [128, 128], replicated, may hold values from -1.5 to 1.5
- radial_bias: float32 [128], replicated, may hold values from -3 to 3
- middle_weight: bfloat16 [128, 128], replicated, may hold values from -0.5 to 0.5
- middle_bias: float32 [128], replicated, may hold values from -3 to 3
- output_weight: float32 [128], replicated, may hold values from -0.5 to 0.5
Outputs:
- atom_energy: float32 [4096, 128], P(('col', 'row'))
- forces: float32 [3, 4096, 128], P(None, ('col', 'row'))
Inputs may be any that keep to these rules, and one draw needn't show every extreme that they name: `factor_panel`: entries above the factor's diagonal are zero.
All inputs are finite; a program needn't handle non-finite values.
Results may differ from a plain program's by a relative error of at most 0.0052.
Values may be sent and summed in bfloat16 or wider, within the bound.
A program may use at most 128 MiB of HBM per device.

v0:
```python
import jax
import jax.numpy as jnp
from jax import lax
from jax.sharding import PartitionSpec as P

TILE = 16


def with_halo(cells, sides, width):
    for axis, dim in sides:
        count = lax.axis_size(axis)
        head = lax.slice_in_dim(cells, 0, width, axis=dim)
        tail = lax.slice_in_dim(cells, cells.shape[dim] - width, cells.shape[dim], axis=dim)
        cells = jnp.concatenate(
            [
                lax.ppermute(tail, axis, [(i, (i + 1) % count) for i in range(count)]),
                cells,
                lax.ppermute(head, axis, [((i + 1) % count, i) for i in range(count)]),
            ],
            axis=dim,
        )
    return cells


def pair_terms(
    own_disp,
    near_disp,
    bond_block,
    radial_weight,
    radial_bias,
    middle_weight,
    middle_bias,
    output_weight,
):
    vectors = bond_block[:, :, :, None] + near_disp - own_disp[:, :, None, :]
    squared = jnp.sum(vectors * vectors, axis=0)
    count = radial_weight.shape[0]
    centres = 30.0 * jnp.arange(count, dtype=jnp.float32) / (count - 1)
    spread = 90.0 / (count - 1)
    scaled = (squared[..., None] - centres) / spread
    basis = jnp.exp(-scaled * scaled)
    flat_basis = basis.reshape(-1, count)
    flat_scaled = scaled.reshape(-1, count)
    first = jnp.tanh(
        jnp.dot(flat_basis.astype(jnp.bfloat16), radial_weight, preferred_element_type=jnp.float32)
        + radial_bias
    )
    second = jnp.tanh(
        jnp.dot(first.astype(jnp.bfloat16), middle_weight, preferred_element_type=jnp.float32)
        + middle_bias
    )
    energies = jnp.sum(second * output_weight, axis=-1)
    back_second = ((1.0 - second * second) * output_weight).astype(jnp.bfloat16)
    back_first = (
        jnp.dot(back_second, middle_weight.T, preferred_element_type=jnp.float32)
        * (1.0 - first * first)
    ).astype(jnp.bfloat16)
    radial_grad = jnp.dot(back_first, radial_weight.T, preferred_element_type=jnp.float32)
    slopes = jnp.sum(radial_grad * flat_basis * (-2.0 / spread) * flat_scaled, axis=-1)
    shape = squared.shape
    atom_part = 0.5 * jnp.sum(energies.reshape(shape), axis=1)
    force_part = 2.0 * jnp.sum(slopes.reshape(shape)[None] * vectors, axis=2)
    return (atom_part, force_part)


def per_device(
    factor_panel,
    normals,
    bond_vectors,
    neighbours,
    send_atoms,
    radial_weight,
    radial_bias,
    middle_weight,
    middle_bias,
    output_weight,
):
    samples = normals.shape[1]
    local_rows = factor_panel.shape[0]
    partial_value = jnp.dot(
        factor_panel,
        lax.all_gather(normals, "row", axis=0, tiled=True),
        preferred_element_type=jnp.float32,
    )
    col_count = lax.axis_size("col")
    col_index = lax.axis_index("col")
    slab_rows = local_rows // col_count
    total = lax.psum(partial_value, "col")
    slab = lax.dynamic_slice_in_dim(total, col_index * slab_rows, slab_rows, 0)
    rows_count = lax.axis_size("row")
    row_index = lax.axis_index("row")
    tiles = slab_rows // TILE
    whole = lax.all_gather(slab, "row", axis=0, tiled=True)
    ordered = (
        whole.reshape(rows_count, tiles, TILE, samples)
        .transpose(1, 0, 2, 3)
        .reshape(rows_count * slab_rows, samples)
    )
    domain = lax.dynamic_slice_in_dim(ordered, row_index * slab_rows, slab_rows, 0)
    domain_atoms = bond_vectors.shape[1]
    neighbour_count = bond_vectors.shape[2]
    displacements = domain.reshape(3, domain_atoms, samples)
    sent = jnp.take(displacements, send_atoms[0], axis=1)
    beside_all = with_halo(sent[None, None], (("row", 0), ("col", 1)), 1)
    halo_atoms = jnp.moveaxis(beside_all, 2, 0).reshape(3, 9 * sent.shape[1], samples)
    pool = jnp.concatenate([displacements, halo_atoms], axis=1)
    nearby = jnp.take(pool, neighbours.reshape(-1), axis=1).reshape(
        3, domain_atoms, neighbour_count, samples
    )
    block_count = domain_atoms // 8
    own_blocks = displacements.reshape(3, block_count, 8, samples).transpose(1, 0, 2, 3)
    near_blocks = nearby.reshape(3, block_count, 8, neighbour_count, samples).transpose(
        1, 0, 2, 3, 4
    )
    bond_blocks = bond_vectors.reshape(3, block_count, 8, neighbour_count).transpose(1, 0, 2, 3)
    energy_blocks, force_blocks = lax.map(
        lambda items: pair_terms(
            items[0],
            items[1],
            items[2],
            radial_weight,
            radial_bias,
            middle_weight,
            middle_bias,
            output_weight,
        ),
        (own_blocks, near_blocks, bond_blocks),
    )
    atom_energy = energy_blocks.reshape(domain_atoms, samples)
    forces = force_blocks.transpose(1, 0, 2, 3).reshape(3, domain_atoms, samples)
    return (atom_energy, forces)


def solution(mesh):
    return jax.shard_map(
        per_device,
        mesh=mesh,
        in_specs=(
            P("row", "col"),
            P(("col", "row"), None),
            P(None, ("col", "row"), None),
            P(("col", "row"), None),
            P(("col", "row"), None),
            P(),
            P(),
            P(),
            P(),
            P(),
        ),
        out_specs=(P(("col", "row"), None), P(None, ("col", "row"), None)),
        check_vma=False,
    )
```

profile of v0, /device:TPU:103, one launch (start us, length us, event | category | flops | bytes accessed | tf_op | source)
XLA Modules:
  0.0 323.6 jit_solution(1270470169724800918)
XLA Ops:
  8.0 35.4 %all-gather.2.cloned.1.call-done = bf16[6144,128]{1,0:T(8,128)(2,1)} async-done(((bf16[768,128]{1,0:T(8,128)(2,1)}), bf16[6144,128]{1,0:T(8,128)(2,1)}) %all-gather.2.cloned.1.call-update) | async-done | bytes 1572880 | tf_op jit(solution)/shard_map/all_gather | solution.py:82
  43.4 10.2 %fusion.22 = f32[1536,128]{1,0:T(8,128)} fusion(bf16[1536,6144]{1,0:T(8,128)(2,1)} %param.12, bf16[6144,128]{1,0:T(8,128)(2,1)} %all-gather.2.cloned.1.call-done), kind=kOutput, calls=%fused_computation.54 | convolution fusion | flops 2415919104 | bytes 21233664 | tf_op jit(solution)/shard_map/dot_general | solution.py:80
  53.9 147.7 %all-reduce.2.cloned.1.call-done = f32[1536,128]{1,0:T(8,128)} async-done(((f32[1536,128]{1,0:T(8,128)}), f32[1536,128]{1,0:T(8,128)}) %all-reduce.2.cloned.1.call-update) | async-done | bytes 786448 | tf_op jit(solution)/shard_map/psum | solution.py:88
  202.4 22.9 %all_gather.7 = f32[768,128]{1,0:T(8,128)S(1)} all-gather(f32[96,128]{1,0:T(8,128)S(1)} %constant_dynamic-slice_fusion.1), channel_id=1, replica_groups=mesh['row'=8,'col'=16] {'row'}, dimensions={0}, use_global_device_ids=true | all-gather | bytes 442368 | tf_op jit(solution)/shard_map/all_gather | solution.py:93
  226.1 0.9 collective-permute-start
  227.8 1.2 collective-permute-done
  228.9 2.9 collective-permute-done.1
  231.9 9.4 %collective-permute-start.2 = (f32[3,1,3,16,128]{4,2,3,1,0:T(4,128)S(1)}, f32[3,1,3,16,128]{4,2,3,1,0:T(4,128)S(1)}, u32[]{:S(2)}, u32[]{:S(2)}) collective-permute-start(f32[3,1,3,16,128]{4,2,3,1,0:T(4,128)S(1)} %pad_maximum_fusion.2), channel_id=1, source_target_pairs={{0,1},{1,2},{2,3},{3,4},{4,5},{5,6},{6,7},{7,8},{8,9},{9,10},{10,1... | collective-permute-start | bytes 221192 | tf_op jit(solution)/shard_map/ppermute | solution.py:16
  241.3 1.6 collective-permute-done.2
  242.9 6.0 %collective-permute-done.3 = f32[3,1,3,16,128]{4,2,3,1,0:T(4,128)S(1)} collective-permute-done((f32[3,1,3,16,128]{4,2,3,1,0:T(4,128)S(1)}, f32[3,1,3,16,128]{4,2,3,1,0:T(4,128)S(1)}, u32[]{:S(2)}, u32[]{:S(2)}) %collective-permute-start.3) | collective-permute-done | bytes 73760 | tf_op jit(solution)/shard_map/ppermute | solution.py:18
  249.1 2.0 gather_fusion.1
  251.4 64.7 %while.14 = (s32[]{:T(128)}, f32[4,8,128]{2,1,0:T(8,128)S(1)}, f32[4,3,8,128]{3,2,1,0:T(8,128)S(1)}, f32[4,3,8,12]{3,2,0,1:T(8,128)S(1)}, f32[4,3,8,12,128]{4,3,...) while((s32[]{:T(128)}, f32[4,8,128]{2,1,0:T(8,128)S(1)}, ...), condition=%wide.region_7.8_spmd, body=%wide.region_1.7_spmd.sunk | while | flops 1651777664 | bytes 57794740 | solution.py:116
  251.6 2.5 fusion.42
  254.0 4.5 %multiply_reduce_fusion.7 = (f32[12288]{0:T(1024)S(1)}, f32[12288,128]{1,0:T(8,128)}) fusion(f32[128]{0:T(128)S(1)} %get-tuple-element.295, f32[128]{0:T(128)S(1)} %get-tuple-element.294, bf16[128,128]{1,0:T(8,128)(2,1)S(1)} %get-tuple-element.293, f32[12288,128]{1,0:T(8,128)S(1)} %fusion.42), kind=kOutput, calls=%fused_computation.15.clone.1 | convolution fusion | flops 408932352 | bytes 12665856 | tf_op jit(solution)/shard_map/while/body/eval_jaxpr/dot_general | solution.py:49
  258.6 8.7 %fusion.43 = f32[12288]{0:T(1024)S(1)} fusion(f32[128]{0:T(128)S(1)} %iota_multiply_fusion.2, f32[12288]{0:T(1024)S(1)} %sub.114, bf16[128,128]{1,0:T(8,128)(2,1)S(1)} %get-tuple-element.291, bf16[128,128]{1,0:T(8,128)(2,1)S(1)} %get-tuple-element.293, f32[12288,128]{1,0:T(8,128)} %copy-done, f32[12288,128]{1,0:T(8,128)} %get-tuple-element.258, ...), kind=kOutput, calls=%fused_computation.23.clone.1 | convolution fusion | flops 830459904 | bytes 12747776 | tf_op jit(solution)/shard_map/while/body/eval_jaxpr/dot_general | solution.py:58
  267.8 2.5 fusion.42
  270.2 4.5 %multiply_reduce_fusion.7 = (f32[12288]{0:T(1024)S(1)}, f32[12288,128]{1,0:T(8,128)}) fusion(f32[128]{0:T(128)S(1)} %get-tuple-element.295, f32[128]{0:T(128)S(1)} %get-tuple-element.294, bf16[128,128]{1,0:T(8,128)(2,1)S(1)} %get-tuple-element.293, f32[12288,128]{1,0:T(8,128)S(1)} %fusion.42), kind=kOutput, calls=%fused_computation.15.clone.1 | convolution fusion | flops 408932352 | bytes 12665856 | tf_op jit(solution)/shard_map/while/body/eval_jaxpr/dot_general | solution.py:49
  274.8 8.7 %fusion.43 = f32[12288]{0:T(1024)S(1)} fusion(f32[128]{0:T(128)S(1)} %iota_multiply_fusion.2, f32[12288]{0:T(1024)S(1)} %sub.114, bf16[128,128]{1,0:T(8,128)(2,1)S(1)} %get-tuple-element.291, bf16[128,128]{1,0:T(8,128)(2,1)S(1)} %get-tuple-element.293, f32[12288,128]{1,0:T(8,128)} %copy-done, f32[12288,128]{1,0:T(8,128)} %get-tuple-element.258, ...), kind=kOutput, calls=%fused_computation.23.clone.1 | convolution fusion | flops 830459904 | bytes 12747776 | tf_op jit(solution)/shard_map/while/body/eval_jaxpr/dot_general | solution.py:58
  283.9 2.5 fusion.42
  286.4 4.5 %multiply_reduce_fusion.7 = (f32[12288]{0:T(1024)S(1)}, f32[12288,128]{1,0:T(8,128)}) fusion(f32[128]{0:T(128)S(1)} %get-tuple-element.295, f32[128]{0:T(128)S(1)} %get-tuple-element.294, bf16[128,128]{1,0:T(8,128)(2,1)S(1)} %get-tuple-element.293, f32[12288,128]{1,0:T(8,128)S(1)} %fusion.42), kind=kOutput, calls=%fused_computation.15.clone.1 | convolution fusion | flops 408932352 | bytes 12665856 | tf_op jit(solution)/shard_map/while/body/eval_jaxpr/dot_general | solution.py:49
  290.9 8.7 %fusion.43 = f32[12288]{0:T(1024)S(1)} fusion(f32[128]{0:T(128)S(1)} %iota_multiply_fusion.2, f32[12288]{0:T(1024)S(1)} %sub.114, bf16[128,128]{1,0:T(8,128)(2,1)S(1)} %get-tuple-element.291, bf16[128,128]{1,0:T(8,128)(2,1)S(1)} %get-tuple-element.293, f32[12288,128]{1,0:T(8,128)} %copy-done, f32[12288,128]{1,0:T(8,128)} %get-tuple-element.258, ...), kind=kOutput, calls=%fused_computation.23.clone.1 | convolution fusion | flops 830459904 | bytes 12747776 | tf_op jit(solution)/shard_map/while/body/eval_jaxpr/dot_general | solution.py:58
  300.1 2.5 fusion.42
  302.6 4.5 %multiply_reduce_fusion.7 = (f32[12288]{0:T(1024)S(1)}, f32[12288,128]{1,0:T(8,128)}) fusion(f32[128]{0:T(128)S(1)} %get-tuple-element.295, f32[128]{0:T(128)S(1)} %get-tuple-element.294, bf16[128,128]{1,0:T(8,128)(2,1)S(1)} %get-tuple-element.293, f32[12288,128]{1,0:T(8,128)S(1)} %fusion.42), kind=kOutput, calls=%fused_computation.15.clone.1 | convolution fusion | flops 408932352 | bytes 12665856 | tf_op jit(solution)/shard_map/while/body/eval_jaxpr/dot_general | solution.py:49
  307.1 8.7 %fusion.43 = f32[12288]{0:T(1024)S(1)} fusion(f32[128]{0:T(128)S(1)} %iota_multiply_fusion.2, f32[12288]{0:T(1024)S(1)} %sub.114, bf16[128,128]{1,0:T(8,128)(2,1)S(1)} %get-tuple-element.291, bf16[128,128]{1,0:T(8,128)(2,1)S(1)} %get-tuple-element.293, f32[12288,128]{1,0:T(8,128)} %copy-done, f32[12288,128]{1,0:T(8,128)} %get-tuple-element.258, ...), kind=kOutput, calls=%fused_computation.23.clone.1 | convolution fusion | flops 830459904 | bytes 12747776 | tf_op jit(solution)/shard_map/while/body/eval_jaxpr/dot_general | solution.py:58
  (98 shorter events, 5.7 us)
Async XLA Ops:
  7.2 36.2 %all-gather.2.cloned.1.call-start = ((), (), s32[]{:S(2)}) async-start(), calls=%async_computation | async-start | bytes 1769472 | tf_op jit(solution)/shard_map/all_gather | solution.py:82
  7.9 45.7 %copy-start.5 = (s32[32,12]{0,1:T(8,128)S(1)}, s32[32,12]{0,1:T(8,128)}, u32[]{:S(2)}) copy-start(s32[32,12]{0,1:T(8,128)} %param.15) | copy-start | bytes 4612
  7.9 45.9 %copy-start.8 = (s32[1,16]{1,0:T(1,128)S(1)}, s32[1,16]{1,0:T(1,128)}, u32[]{:S(2)}) copy-start(s32[1,16]{1,0:T(1,128)} %param.16) | copy-start | bytes 196
  7.9 219.7 %copy-start.2 = (f32[3,32,12]{1,2,0:T(8,128)S(1)}, f32[3,32,12]{1,2,0:T(8,128)}, u32[]{:S(2)}) copy-start(f32[3,32,12]{1,2,0:T(8,128)} %param.14) | copy-start | bytes 13828
  7.9 193.6 %all-reduce.2.cloned.1.call-start = ((), (), s32[]{:S(2)}) async-start(), calls=%async_computation.1 | async-start | bytes 1572864 | tf_op jit(solution)/shard_map/psum | solution.py:88
  53.6 197.7 %copy-start.1 = (bf16[128,128]{1,0:T(8,128)(2,1)S(1)}, bf16[128,128]{1,0:T(8,128)(2,1)}, u32[]{:S(2)}) copy-start(bf16[128,128]{1,0:T(8,128)(2,1)} %param.19) | copy-start | bytes 98308
  53.6 197.8 %copy-start.3 = (f32[128]{0:T(128)S(1)}, f32[128]{0:T(128)}, u32[]{:S(2)}) copy-start(f32[128]{0:T(128)} %param.20) | copy-start | bytes 1540
  53.6 197.8 %copy-start.4 = (f32[128]{0:T(128)S(1)}, f32[128]{0:T(128)}, u32[]{:S(2)}) copy-start(f32[128]{0:T(128)} %param.21) | copy-start | bytes 1540
  53.6 197.8 %copy-start.6 = (bf16[128,128]{1,0:T(8,128)(2,1)S(1)}, bf16[128,128]{1,0:T(8,128)(2,1)}, u32[]{:S(2)}) copy-start(bf16[128,128]{1,0:T(8,128)(2,1)} %param.17) | copy-start | bytes 98308
  53.6 197.8 %copy-start.9 = (f32[128]{0:T(128)S(1)}, f32[128]{0:T(128)}, u32[]{:S(2)}) copy-start(f32[128]{0:T(128)} %param.18) | copy-start | bytes 1540
  226.1 2.8 collective-permute-start
  227.0 4.9 %collective-permute-start.1 = (f32[1,1,3,16,128]{4,2,3,1,0:T(4,128)S(1)}, f32[1,1,3,16,128]{4,2,3,1,0:T(4,128)S(1)}, u32[]{:S(2)}, u32[]{:S(2)}) collective-permute-start(f32[1,1,3,16,128]{4,2,3,1,0:T(4,128)S(1)} %bitcast_select_fusion), channel_id=1, source_target_pairs={{16,0},{32,16},{48,32},{64,48},{80,64},{96,80},{112,96},{0,112},{1... | collective-permute-start | bytes 73736 | tf_op jit(solution)/shard_map/ppermute | solution.py:18
  231.9 11.0 %collective-permute-start.2 = (f32[3,1,3,16,128]{4,2,3,1,0:T(4,128)S(1)}, f32[3,1,3,16,128]{4,2,3,1,0:T(4,128)S(1)}, u32[]{:S(2)}, u32[]{:S(2)}) collective-permute-start(f32[3,1,3,16,128]{4,2,3,1,0:T(4,128)S(1)} %pad_maximum_fusion.2), channel_id=1, source_target_pairs={{0,1},{1,2},{2,3},{3,4},{4,5},{5,6},{6,7},{7,8},{8,9},{9,10},{10,1... | collective-permute-start | bytes 221192 | tf_op jit(solution)/shard_map/ppermute | solution.py:16
  241.3 7.7 %collective-permute-start.3 = (f32[3,1,3,16,128]{4,2,3,1,0:T(4,128)S(1)}, f32[3,1,3,16,128]{4,2,3,1,0:T(4,128)S(1)}, u32[]{:S(2)}, u32[]{:S(2)}) collective-permute-start(f32[3,1,3,16,128]{4,2,3,1,0:T(4,128)S(1)} %pad_maximum_fusion.2), channel_id=1, source_target_pairs={{1,0},{2,1},{3,2},{4,3},{5,4},{6,5},{7,6},{8,7},{9,8},{10,9},{11,1... | collective-permute-start | bytes 221192 | tf_op jit(solution)/shard_map/ppermute | solution.py:18
  254.0 4.5 %copy-start = (f32[12288,128]{1,0:T(8,128)}, f32[12288,128]{1,0:T(8,128)S(1)}, u32[]{:S(2)}) copy-start(f32[12288,128]{1,0:T(8,128)S(1)} %fusion.42) | copy-start | bytes 18874372 | tf_op jit(solution)/shard_map/while
  270.2 4.5 %copy-start = (f32[12288,128]{1,0:T(8,128)}, f32[12288,128]{1,0:T(8,128)S(1)}, u32[]{:S(2)}) copy-start(f32[12288,128]{1,0:T(8,128)S(1)} %fusion.42) | copy-start | bytes 18874372 | tf_op jit(solution)/shard_map/while
  286.4 4.5 %copy-start = (f32[12288,128]{1,0:T(8,128)}, f32[12288,128]{1,0:T(8,128)S(1)}, u32[]{:S(2)}) copy-start(f32[12288,128]{1,0:T(8,128)S(1)} %fusion.42) | copy-start | bytes 18874372 | tf_op jit(solution)/shard_map/while
  302.6 4.5 %copy-start = (f32[12288,128]{1,0:T(8,128)}, f32[12288,128]{1,0:T(8,128)S(1)}, u32[]{:S(2)}) copy-start(f32[12288,128]{1,0:T(8,128)S(1)} %fusion.42) | copy-start | bytes 18874372 | tf_op jit(solution)/shard_map/while
  316.1 0.6 copy-start.7
Sparse Core Ops, SparseCore 0:
  9.6 33.7 all-gather.1
  53.8 147.7 all-reduce.1
where the time goes:
time: 324 us
  waiting for transfers between devices  196 us (60%)
  matrix products  73.1 us (23%)
  blocking collectives  22.9 us (7%)
  between operations  14.3 us (4%)
  starting transfers between devices  11 us (3%)
  local copies, waits for them, and re-layouts  4.61 us (1%)
    psum x1, waiting for transfers between devices, per_device(): total = lax.psum(partial_value, 'col')  148 us
    all_gather x1, waiting for transfers between devices, per_device(): lax.all_gather(normals, 'row', axis=0, tiled=True)  35.4 us
    dot_general x4, matrix products, pair_terms(): jnp.dot(back_first, radial_weight.T, preferred_element_type=jnp.float32)  35 us
    all_gather x1, blocking collectives, per_device(): whole = lax.all_gather(slab, 'row', axis=0, tiled=True)  22.9 us
    dot_general x4, matrix products, pair_terms(): jnp.dot(first.astype(jnp.bfloat16), middle_weight, preferred_element_type...  18.1 us
    ppermute x2, starting transfers between devices, with_halo(): lax.ppermute(tail, axis, [(i, (i + 1) % count) for i in range(count)])  10.3 us
    dot_general x1, matrix products, per_device(): jnp.dot(factor_panel, lax.all_gather(normals, 'row', axis=0, tiled=True),...  10.2 us
    dot_general x4, matrix products, pair_terms(): jnp.dot(flat_basis.astype(jnp.bfloat16), radial_weight, preferred_element...  9.83 us
  transfers between devices with their start and end apart: 6, of which 6 were waited for; matrix products, arithmetic and copies ran while one was open for 0% of the time, Pallas kernels for 0%

commit v1 on v0

--- a/solution.py
+++ b/solution.py
@@ -85,7 +85,7 @@
     col_count = lax.axis_size("col")
     col_index = lax.axis_index("col")
     slab_rows = local_rows // col_count
-    total = lax.psum(partial_value, "col")
+    total = jnp.sum(lax.all_gather(partial_value, "col"), axis=0)
     slab = lax.dynamic_slice_in_dim(total, col_index * slab_rows, slab_rows, 0)
     rows_count = lax.axis_size("row")
     row_index = lax.axis_index("row")

time: 324 us -> 277 us (0.85)
  waiting for transfers between devices: 196 us -> 143 us
  other arithmetic: 1.69 us -> 6.96 us
    psum x1 -> x0, waiting for transfers between devices: 148 us -> none  [per_device(): total = lax.psum(partial_value, 'col')]
    all_gather x0 -> x1, waiting for transfers between devices: none -> 95.5 us  [per_device(): total = jnp.sum(lax.all_gather(partial_value, 'col'), axis=0)]
    reduce_sum x0 -> x1, other arithmetic: none -> 5.27 us  [per_device(): total = jnp.sum(lax.all_gather(partial_value, 'col'), axis=0)]
where the time goes in v1:
time: 277 us
  waiting for transfers between devices  143 us (52%)
  matrix products  72.9 us (26%)
  blocking collectives  22.6 us (8%)
  between operations  14.3 us (5%)
  starting transfers between devices  12.6 us (5%)
  other arithmetic  6.96 us (3%)
  local copies, waits for them, and re-layouts  3.82 us (1%)
    all_gather x1, waiting for transfers between devices, per_device(): total = jnp.sum(lax.all_gather(partial_value, 'col'), axis=0)  95.5 us
    all_gather x1, waiting for transfers between devices, per_device(): lax.all_gather(normals, 'row', axis=0, tiled=True)  35.4 us
    dot_general x4, matrix products, pair_terms(): jnp.dot(back_first, radial_weight.T, preferred_element_type=jnp.float32)  34.9 us
    all_gather x1, blocking collectives, per_device(): whole = lax.all_gather(slab, 'row', axis=0, tiled=True)  22.6 us
    dot_general x4, matrix products, pair_terms(): jnp.dot(first.astype(jnp.bfloat16), middle_weight, preferred_element_type...  18.1 us
    ppermute x2, starting transfers between devices, with_halo(): lax.ppermute(tail, axis, [(i, (i + 1) % count) for i in range(count)])  11.8 us
    dot_general x1, matrix products, per_device(): jnp.dot(factor_panel, lax.all_gather(normals, 'row', axis=0, tiled=True),...  10.2 us
    dot_general x4, matrix products, pair_terms(): jnp.dot(flat_basis.astype(jnp.bfloat16), radial_weight, preferred_element...  9.82 us
  transfers between devices with their start and end apart: 6, of which 6 were waited for; matrix products, arithmetic and copies ran while one was open for 0% of the time, Pallas kernels for 0%

profile of v1, /device:TPU:103, one launch (start us, length us, event | category | flops | bytes accessed | tf_op | source)
XLA Modules:
  0.0 277.0 jit_solution(8521612550738920961)
XLA Ops:
  8.0 35.4 %all-gather.4.cloned.1.call-done = bf16[6144,128]{1,0:T(8,128)(2,1)} async-done(((bf16[768,128]{1,0:T(8,128)(2,1)}), bf16[6144,128]{1,0:T(8,128)(2,1)}) %all-gather.4.cloned.1.call-update) | async-done | bytes 1572880 | tf_op jit(solution)/shard_map/all_gather | solution.py:82
  43.4 10.2 %fusion.22 = f32[1536,128]{1,0:T(8,128)} fusion(bf16[1536,6144]{1,0:T(8,128)(2,1)} %param.12, bf16[6144,128]{1,0:T(8,128)(2,1)} %all-gather.4.cloned.1.call-done), kind=kOutput, calls=%fused_computation.54 | convolution fusion | flops 2415919104 | bytes 21233664 | tf_op jit(solution)/shard_map/dot_general | solution.py:80
  53.9 95.5 %all-gather.6.cloned.1.call-done = f32[24576,128]{1,0:T(8,128)} async-done(((f32[1536,128]{1,0:T(8,128)}), f32[24576,128]{1,0:T(8,128)}) %all-gather.6.cloned.1.call-update) | async-done | bytes 12582928 | tf_op jit(solution)/shard_map/all_gather | solution.py:88
  149.4 5.3 %reduce_sum.69 = f32[1536,128]{1,0:T(8,128)S(1)} reduce(f32[16,1536,128]{2,1,0:T(8,128)} %bitcast.88, f32[]{:T(128)} %constant.102.clone.1), dimensions={0}, to_apply=%region_0.0 | reduce | flops 2949120 | bytes 13369348 | tf_op jit(solution)/shard_map/reduce_sum | solution.py:88
  154.7 22.6 %all_gather.15 = f32[768,128]{1,0:T(8,128)S(1)} all-gather(f32[96,128]{1,0:T(8,128)S(1)} %constant_dynamic-slice_fusion.1), channel_id=1, replica_groups=mesh['row'=8,'col'=16] {'row'}, dimensions={0}, use_global_device_ids=true | all-gather | bytes 442368 | tf_op jit(solution)/shard_map/all_gather | solution.py:93
  179.8 1.6 collective-permute-done
  181.4 2.4 collective-permute-done.1
  183.8 11.0 %collective-permute-start.2 = (f32[3,1,3,16,128]{4,2,3,1,0:T(4,128)S(1)}, f32[3,1,3,16,128]{4,2,3,1,0:T(4,128)S(1)}, u32[]{:S(2)}, u32[]{:S(2)}) collective-permute-start(f32[3,1,3,16,128]{4,2,3,1,0:T(4,128)S(1)} %pad_maximum_fusion.2), channel_id=1, source_target_pairs={{0,1},{1,2},{2,3},{3,4},{4,5},{5,6},{6,7},{7,8},{8,9},{9,10},{10,1... | collective-permute-start | bytes 221192 | tf_op jit(solution)/shard_map/ppermute | solution.py:16
  194.8 1.6 collective-permute-done.2
  196.5 6.0 %collective-permute-done.3 = f32[3,1,3,16,128]{4,2,3,1,0:T(4,128)S(1)} collective-permute-done((f32[3,1,3,16,128]{4,2,3,1,0:T(4,128)S(1)}, f32[3,1,3,16,128]{4,2,3,1,0:T(4,128)S(1)}, u32[]{:S(2)}, u32[]{:S(2)}) %collective-permute-start.3) | collective-permute-done | bytes 73760 | tf_op jit(solution)/shard_map/ppermute | solution.py:18
  202.6 2.0 gather_fusion.1
  204.9 64.6 %while.14 = (s32[]{:T(128)}, f32[4,8,128]{2,1,0:T(8,128)S(1)}, f32[4,3,8,128]{3,2,1,0:T(8,128)S(1)}, f32[4,3,8,12]{3,2,0,1:T(8,128)S(1)}, f32[4,3,8,12,128]{4,3,...) while((s32[]{:T(128)}, f32[4,8,128]{2,1,0:T(8,128)S(1)}, ...), condition=%wide.region_7.8_spmd, body=%wide.region_1.7_spmd.sunk | while | flops 1651777664 | bytes 57794740 | solution.py:116
  205.1 2.5 fusion.42
  207.6 4.5 %multiply_reduce_fusion.7 = (f32[12288]{0:T(1024)S(1)}, f32[12288,128]{1,0:T(8,128)}) fusion(f32[128]{0:T(128)S(1)} %get-tuple-element.295, f32[128]{0:T(128)S(1)} %get-tuple-element.294, bf16[128,128]{1,0:T(8,128)(2,1)S(1)} %get-tuple-element.293, f32[12288,128]{1,0:T(8,128)S(1)} %fusion.42), kind=kOutput, calls=%fused_computation.15.clone.1 | convolution fusion | flops 408932352 | bytes 12665856 | tf_op jit(solution)/shard_map/while/body/eval_jaxpr/dot_general | solution.py:49
  212.1 8.7 %fusion.43 = f32[12288]{0:T(1024)S(1)} fusion(f32[128]{0:T(128)S(1)} %iota_multiply_fusion.2, f32[12288]{0:T(1024)S(1)} %sub.114, bf16[128,128]{1,0:T(8,128)(2,1)S(1)} %get-tuple-element.291, bf16[128,128]{1,0:T(8,128)(2,1)S(1)} %get-tuple-element.293, f32[12288,128]{1,0:T(8,128)} %copy-done, f32[12288,128]{1,0:T(8,128)} %get-tuple-element.258, ...), kind=kOutput, calls=%fused_computation.23.clone.1 | convolution fusion | flops 830459904 | bytes 12747776 | tf_op jit(solution)/shard_map/while/body/eval_jaxpr/dot_general | solution.py:58
  221.2 2.5 fusion.42
  223.7 4.5 %multiply_reduce_fusion.7 = (f32[12288]{0:T(1024)S(1)}, f32[12288,128]{1,0:T(8,128)}) fusion(f32[128]{0:T(128)S(1)} %get-tuple-element.295, f32[128]{0:T(128)S(1)} %get-tuple-element.294, bf16[128,128]{1,0:T(8,128)(2,1)S(1)} %get-tuple-element.293, f32[12288,128]{1,0:T(8,128)S(1)} %fusion.42), kind=kOutput, calls=%fused_computation.15.clone.1 | convolution fusion | flops 408932352 | bytes 12665856 | tf_op jit(solution)/shard_map/while/body/eval_jaxpr/dot_general | solution.py:49
  228.2 8.7 %fusion.43 = f32[12288]{0:T(1024)S(1)} fusion(f32[128]{0:T(128)S(1)} %iota_multiply_fusion.2, f32[12288]{0:T(1024)S(1)} %sub.114, bf16[128,128]{1,0:T(8,128)(2,1)S(1)} %get-tuple-element.291, bf16[128,128]{1,0:T(8,128)(2,1)S(1)} %get-tuple-element.293, f32[12288,128]{1,0:T(8,128)} %copy-done, f32[12288,128]{1,0:T(8,128)} %get-tuple-element.258, ...), kind=kOutput, calls=%fused_computation.23.clone.1 | convolution fusion | flops 830459904 | bytes 12747776 | tf_op jit(solution)/shard_map/while/body/eval_jaxpr/dot_general | solution.py:58
  237.4 2.5 fusion.42
  239.9 4.5 %multiply_reduce_fusion.7 = (f32[12288]{0:T(1024)S(1)}, f32[12288,128]{1,0:T(8,128)}) fusion(f32[128]{0:T(128)S(1)} %get-tuple-element.295, f32[128]{0:T(128)S(1)} %get-tuple-element.294, bf16[128,128]{1,0:T(8,128)(2,1)S(1)} %get-tuple-element.293, f32[12288,128]{1,0:T(8,128)S(1)} %fusion.42), kind=kOutput, calls=%fused_computation.15.clone.1 | convolution fusion | flops 408932352 | bytes 12665856 | tf_op jit(solution)/shard_map/while/body/eval_jaxpr/dot_general | solution.py:49
  244.4 8.7 %fusion.43 = f32[12288]{0:T(1024)S(1)} fusion(f32[128]{0:T(128)S(1)} %iota_multiply_fusion.2, f32[12288]{0:T(1024)S(1)} %sub.114, bf16[128,128]{1,0:T(8,128)(2,1)S(1)} %get-tuple-element.291, bf16[128,128]{1,0:T(8,128)(2,1)S(1)} %get-tuple-element.293, f32[12288,128]{1,0:T(8,128)} %copy-done, f32[12288,128]{1,0:T(8,128)} %get-tuple-element.258, ...), kind=kOutput, calls=%fused_computation.23.clone.1 | convolution fusion | flops 830459904 | bytes 12747776 | tf_op jit(solution)/shard_map/while/body/eval_jaxpr/dot_general | solution.py:58
  253.5 2.5 fusion.42
  256.0 4.5 %multiply_reduce_fusion.7 = (f32[12288]{0:T(1024)S(1)}, f32[12288,128]{1,0:T(8,128)}) fusion(f32[128]{0:T(128)S(1)} %get-tuple-element.295, f32[128]{0:T(128)S(1)} %get-tuple-element.294, bf16[128,128]{1,0:T(8,128)(2,1)S(1)} %get-tuple-element.293, f32[12288,128]{1,0:T(8,128)S(1)} %fusion.42), kind=kOutput, calls=%fused_computation.15.clone.1 | convolution fusion | flops 408932352 | bytes 12665856 | tf_op jit(solution)/shard_map/while/body/eval_jaxpr/dot_general | solution.py:49
  260.5 8.7 %fusion.43 = f32[12288]{0:T(1024)S(1)} fusion(f32[128]{0:T(128)S(1)} %iota_multiply_fusion.2, f32[12288]{0:T(1024)S(1)} %sub.114, bf16[128,128]{1,0:T(8,128)(2,1)S(1)} %get-tuple-element.291, bf16[128,128]{1,0:T(8,128)(2,1)S(1)} %get-tuple-element.293, f32[12288,128]{1,0:T(8,128)} %copy-done, f32[12288,128]{1,0:T(8,128)} %get-tuple-element.258, ...), kind=kOutput, calls=%fused_computation.23.clone.1 | convolution fusion | flops 830459904 | bytes 12747776 | tf_op jit(solution)/shard_map/while/body/eval_jaxpr/dot_general | solution.py:58
  (99 shorter events, 5.8 us)
Async XLA Ops:
  7.2 36.2 %all-gather.4.cloned.1.call-start = ((), (), s32[]{:S(2)}) async-start(), calls=%async_computation | async-start | bytes 1769472 | tf_op jit(solution)/shard_map/all_gather | solution.py:82
  7.9 45.7 %copy-start.5 = (s32[32,12]{0,1:T(8,128)S(1)}, s32[32,12]{0,1:T(8,128)}, u32[]{:S(2)}) copy-start(s32[32,12]{0,1:T(8,128)} %param.15) | copy-start | bytes 4612
  7.9 45.9 %copy-start.8 = (s32[1,16]{1,0:T(1,128)S(1)}, s32[1,16]{1,0:T(1,128)}, u32[]{:S(2)}) copy-start(s32[1,16]{1,0:T(1,128)} %param.16) | copy-start | bytes 196
  7.9 141.4 %all-gather.6.cloned.1.call-start = ((), (), s32[]{:S(2)}) async-start(), calls=%async_computation.1 | async-start | bytes 13369344 | tf_op jit(solution)/shard_map/all_gather | solution.py:88
  149.4 30.3 %copy-start.2 = (f32[3,32,12]{1,2,0:T(8,128)S(1)}, f32[3,32,12]{1,2,0:T(8,128)}, u32[]{:S(2)}) copy-start(f32[3,32,12]{1,2,0:T(8,128)} %param.14) | copy-start | bytes 13828
  149.4 55.5 %copy-start.1 = (bf16[128,128]{1,0:T(8,128)(2,1)S(1)}, bf16[128,128]{1,0:T(8,128)(2,1)}, u32[]{:S(2)}) copy-start(bf16[128,128]{1,0:T(8,128)(2,1)} %param.19) | copy-start | bytes 98308
  149.4 55.5 %copy-start.3 = (f32[128]{0:T(128)S(1)}, f32[128]{0:T(128)}, u32[]{:S(2)}) copy-start(f32[128]{0:T(128)} %param.20) | copy-start | bytes 1540
  149.4 55.5 %copy-start.4 = (f32[128]{0:T(128)S(1)}, f32[128]{0:T(128)}, u32[]{:S(2)}) copy-start(f32[128]{0:T(128)} %param.21) | copy-start | bytes 1540
  149.4 55.5 %copy-start.6 = (bf16[128,128]{1,0:T(8,128)(2,1)S(1)}, bf16[128,128]{1,0:T(8,128)(2,1)}, u32[]{:S(2)}) copy-start(bf16[128,128]{1,0:T(8,128)(2,1)} %param.17) | copy-start | bytes 98308
  149.4 55.5 %copy-start.9 = (f32[128]{0:T(128)S(1)}, f32[128]{0:T(128)}, u32[]{:S(2)}) copy-start(f32[128]{0:T(128)} %param.18) | copy-start | bytes 1540
  178.1 3.3 %collective-permute-start = (f32[1,1,3,16,128]{4,2,3,1,0:T(4,128)S(1)}, f32[1,1,3,16,128]{4,2,3,1,0:T(4,128)S(1)}, u32[]{:S(2)}, u32[]{:S(2)}) collective-permute-start(f32[1,1,3,16,128]{4,2,3,1,0:T(4,128)S(1)} %bitcast_select_fusion), channel_id=1, source_target_pairs={{0,16},{16,32},{32,48},{48,64},{64,80},{80,96},{96,112},{112,0},{1... | collective-permute-start | bytes 73736 | tf_op jit(solution)/shard_map/ppermute | solution.py:16
  178.9 4.9 %collective-permute-start.1 = (f32[1,1,3,16,128]{4,2,3,1,0:T(4,128)S(1)}, f32[1,1,3,16,128]{4,2,3,1,0:T(4,128)S(1)}, u32[]{:S(2)}, u32[]{:S(2)}) collective-permute-start(f32[1,1,3,16,128]{4,2,3,1,0:T(4,128)S(1)} %bitcast_select_fusion), channel_id=1, source_target_pairs={{16,0},{32,16},{48,32},{64,48},{80,64},{96,80},{112,96},{0,112},{1... | collective-permute-start | bytes 73736 | tf_op jit(solution)/shard_map/ppermute | solution.py:18
  183.8 12.7 %collective-permute-start.2 = (f32[3,1,3,16,128]{4,2,3,1,0:T(4,128)S(1)}, f32[3,1,3,16,128]{4,2,3,1,0:T(4,128)S(1)}, u32[]{:S(2)}, u32[]{:S(2)}) collective-permute-start(f32[3,1,3,16,128]{4,2,3,1,0:T(4,128)S(1)} %pad_maximum_fusion.2), channel_id=1, source_target_pairs={{0,1},{1,2},{2,3},{3,4},{4,5},{5,6},{6,7},{7,8},{8,9},{9,10},{10,1... | collective-permute-start | bytes 221192 | tf_op jit(solution)/shard_map/ppermute | solution.py:16
  194.8 7.7 %collective-permute-start.3 = (f32[3,1,3,16,128]{4,2,3,1,0:T(4,128)S(1)}, f32[3,1,3,16,128]{4,2,3,1,0:T(4,128)S(1)}, u32[]{:S(2)}, u32[]{:S(2)}) collective-permute-start(f32[3,1,3,16,128]{4,2,3,1,0:T(4,128)S(1)} %pad_maximum_fusion.2), channel_id=1, source_target_pairs={{1,0},{2,1},{3,2},{4,3},{5,4},{6,5},{7,6},{8,7},{9,8},{10,9},{11,1... | collective-permute-start | bytes 221192 | tf_op jit(solution)/shard_map/ppermute | solution.py:18
  207.6 4.5 %copy-start = (f32[12288,128]{1,0:T(8,128)}, f32[12288,128]{1,0:T(8,128)S(1)}, u32[]{:S(2)}) copy-start(f32[12288,128]{1,0:T(8,128)S(1)} %fusion.42) | copy-start | bytes 18874372 | tf_op jit(solution)/shard_map/while
  223.7 4.5 %copy-start = (f32[12288,128]{1,0:T(8,128)}, f32[12288,128]{1,0:T(8,128)S(1)}, u32[]{:S(2)}) copy-start(f32[12288,128]{1,0:T(8,128)S(1)} %fusion.42) | copy-start | bytes 18874372 | tf_op jit(solution)/shard_map/while
  239.9 4.5 %copy-start = (f32[12288,128]{1,0:T(8,128)}, f32[12288,128]{1,0:T(8,128)S(1)}, u32[]{:S(2)}) copy-start(f32[12288,128]{1,0:T(8,128)S(1)} %fusion.42) | copy-start | bytes 18874372 | tf_op jit(solution)/shard_map/while
  256.0 4.5 %copy-start = (f32[12288,128]{1,0:T(8,128)}, f32[12288,128]{1,0:T(8,128)S(1)}, u32[]{:S(2)}) copy-start(f32[12288,128]{1,0:T(8,128)S(1)} %fusion.42) | copy-start | bytes 18874372 | tf_op jit(solution)/shard_map/while
  269.5 0.6 copy-start.7
Sparse Core Ops, SparseCore 0:
  9.6 33.7 all-gather.3
  53.7 95.5 all-gather.5
